TPU v7x, 512 devices: a whole 4x8x8 slice. The times are simulated.
512 devices in a mesh: frame: 64 (over x, z_hi, y), row: 8 (over z_lo, core).
Axes of the slice: x: 4, y: 8, z: 8 (z_hi: 2, z_lo: 4; z = z_hi * 4 + z_lo), core: 2. Of those that a mesh axis runs over, the one named last changes fastest.
Arguments:
- latents: bfloat16 [256, 32, 32, 320], P('frame', 'row'), may hold values from -20 to 20
- ln_gain: bfloat16 [320], replicated, may hold values from 0.099609375 to 1.8984375
- q_weight: bfloat16 [320, 320], replicated, may hold values from -0.30078125 to 0.30078125
- k_weight: bfloat16 [320, 320], replicated, may hold values from -3 to 3
- v_weight: bfloat16 [320, 320], replicated, may hold values from -0.3125 to 0.3125
- o_weight: bfloat16 [320, 320], replicated, may hold values from -0.3125 to 0.3125
- gn_gain: bfloat16 [320], replicated, may hold values from 0.099609375 to 1.8984375
- conv_weight: bfloat16 [3, 3, 320, 320], replicated, may hold values from -0.109375 to 0.109375
- conv_bias: bfloat16 [320], replicated, may hold values from -3 to 3
Outputs:
- output: bfloat16 [256, 32, 32, 320], P('frame', 'row')
All inputs are finite; a program needn't handle non-finite values.
Results may differ from a plain program's by a relative error of at most 0.0085.
The roundings to bfloat16 on the way count: a program that leaves them out, or rounds other values in their place, can miss the bound.
Values may be sent and summed in bfloat16 or wider, within the bound.
A program may use at most 64 MiB of HBM per device.

v0:
```python
import math
import jax
import jax.numpy as jnp
from jax import lax
from jax.sharding import PartitionSpec as P

HEADS = 8
GROUPS = 32


def spread_2(value, axis, source):
    kept = jnp.where(lax.axis_index(axis) == source, value, 0).astype(value.dtype)
    return lax.psum(kept, axis)


def shifted(block, axis, distance):
    devices = range(lax.axis_size(axis))
    route = [(i - distance, i) for i in devices if i - distance in devices]
    return lax.ppermute(block, axis, route)


def with_halo(value, sides, width):
    for axis, dim in sides:
        size, length = (lax.axis_size(axis), value.shape[dim])
        up = [(i, (i + 1) % size) for i in range(size - 1)]
        down = [(j, i) for i, j in up]
        last = lax.slice_in_dim(value, length - width, length, axis=dim)
        leading = lax.slice_in_dim(value, 0, width, axis=dim)
        before = lax.ppermute(last, axis, up)
        after = lax.ppermute(leading, axis, down)
        value = jnp.concatenate([before, value, after], axis=dim)
    return value


def layer_normed(values, gain_vec):
    floated = values.astype(jnp.float32)
    centre = floated - jnp.mean(floated, axis=-1, keepdims=True)
    spread = jnp.mean(centre * centre, axis=-1, keepdims=True)
    return (centre * lax.rsqrt(spread + 1e-05) * gain_vec.astype(jnp.float32)).astype(jnp.bfloat16)


def attend_frames(queries, key_set, value_set, factor):
    lead_keys = key_set[0]
    lead_values = value_set[0]

    def single(operands):
        frame_queries, frame_keys, frame_values = operands
        all_keys = jnp.concatenate([lead_keys, frame_keys], axis=0)
        all_values = jnp.concatenate([lead_values, frame_values], axis=0)
        scores = (
            jnp.einsum("qhd,khd->hqk", frame_queries, all_keys, preferred_element_type=jnp.float32)
            * factor
        )
        highest = jnp.max(scores, axis=-1, keepdims=True)
        raised = jnp.exp(scores - highest)
        totals = jnp.sum(raised, axis=-1)
        summed = jnp.einsum(
            "hqk,khd->qhd",
            raised.astype(jnp.bfloat16),
            all_values,
            preferred_element_type=jnp.float32,
        )
        return (summed / jnp.transpose(totals)[:, :, None]).astype(jnp.bfloat16)

    return lax.map(single, (queries, key_set[1:], value_set[1:]))


def body(latents, ln_gain, q_weight, k_weight, v_weight, o_weight, gn_gain, conv_weight, conv_bias):
    frames, row_count, col_count, channels = latents.shape
    tok_shard = row_count * col_count
    head_dim = channels // HEADS
    factor = 1.0 / math.sqrt(head_dim)
    tokens = latents.reshape(frames * tok_shard, channels)
    kv_weight = jnp.concatenate([k_weight, v_weight], axis=1)
    normed = layer_normed(tokens, ln_gain)
    queries = jnp.dot(normed, q_weight, preferred_element_type=jnp.float32).astype(jnp.bfloat16)
    queries = queries.reshape(frames, tok_shard, channels)
    paired = jnp.dot(normed, kv_weight, preferred_element_type=jnp.float32).astype(jnp.bfloat16)
    paired = paired.reshape(frames, tok_shard, 2 * channels)
    leading = spread_2(paired[0], "frame", 0)
    earlier = shifted(paired[frames - 1], "frame", 1)
    earlier = jnp.where(lax.axis_index("frame") == 0, paired[0], earlier)
    stacked = jnp.concatenate([leading[None], earlier[None], paired[: frames - 1]], axis=0)
    sent_queries = queries.reshape(frames, tok_shard, 1, HEADS, head_dim)
    sent_pairs = stacked.reshape(frames + 1, tok_shard, 2, HEADS, head_dim)
    got_queries, got_pairs = (
        lax.all_to_all(sent_queries, "row", split_axis=3, concat_axis=1, tiled=True),
        lax.all_to_all(sent_pairs, "row", split_axis=3, concat_axis=1, tiled=True),
    )
    head_results = attend_frames(
        got_queries[:, :, 0], got_pairs[:, :, 0], got_pairs[:, :, 1], factor
    )
    returned = lax.all_to_all(head_results, "row", split_axis=1, concat_axis=2, tiled=True)
    attended = returned.reshape(frames * tok_shard, channels)
    mixed = jnp.dot(attended, o_weight, preferred_element_type=jnp.float32)
    updated = (tokens.astype(jnp.float32) + mixed).astype(jnp.bfloat16)
    group_width = channels // GROUPS
    grouped = updated.astype(jnp.float32).reshape(frames, tok_shard, GROUPS, group_width)
    sum_parts = jnp.sum(grouped, axis=(1, 3))
    square_parts = jnp.sum(grouped * grouped, axis=(1, 3))
    group_sum, group_square = lax.psum((sum_parts, square_parts), "row")
    counted = tok_shard * lax.axis_size("row") * group_width
    group_mean = group_sum / counted
    group_var = group_square / counted - group_mean * group_mean
    scaled = (grouped - group_mean[:, None, :, None]) * lax.rsqrt(group_var + 1e-05)[
        :, None, :, None
    ]
    activated = jax.nn.silu(
        scaled.reshape(frames, tok_shard, channels) * gn_gain.astype(jnp.float32)
    )
    activated = activated.astype(jnp.bfloat16).reshape(frames, row_count, col_count, channels)
    padded = with_halo(activated, (("row", 1),), 1)
    padded = jnp.pad(padded, ((0, 0), (0, 0), (1, 1), (0, 0)))
    convolved = jnp.zeros((frames * tok_shard, channels), jnp.float32)
    for row_off in range(3):
        for col_off in range(3):
            window = padded[
                :, row_off : row_off + row_count, col_off : col_off + col_count, :
            ].reshape(frames * tok_shard, channels)
            convolved = convolved + jnp.dot(
                window, conv_weight[row_off, col_off], preferred_element_type=jnp.float32
            )
    output = updated.astype(jnp.float32) + convolved + conv_bias.astype(jnp.float32)
    return output.astype(jnp.bfloat16).reshape(frames, row_count, col_count, channels)


def solution(mesh):
    in_specs = (P("frame", "row", None, None), P(), P(), P(), P(), P(), P(), P(), P())
    out_specs = P("frame", "row", None, None)
    return jax.shard_map(body, mesh=mesh, in_specs=in_specs, out_specs=out_specs, check_vma=False)
```

profile of v0, /device:TPU:1, one launch (start us, length us, event | category | flops | bytes accessed | tf_op | source)
XLA Modules:
  0.0 901.8 jit_solution(13939154227271930684)
XLA Ops:
  6.5 1.2 convert_reduce_fusion
  7.8 1.3 multiply_reduce_fusion.1
  9.2 0.7 convert_element_type.63
  9.9 1.2 multiply_convert_fusion.1
  11.1 0.4 convolution_convert_fusion.1
  11.6 0.8 copy.107
  12.4 10.2 %all-to-all-start.1 = ((bf16[4,128,1,8,40]{1,4,0,2,3:T(8,128)(2,1)}), bf16[4,128,1,8,40]{1,4,0,2,3:T(8,128)(2,1)S(1)}, u32[]{:S(2)}, u32[]{:S(2)}) async-start(bf16[4,128,1,8,40]{1,4,0,2,3:T(8,128)(2,1)} %copy.107), calls=%async_computation.1 | async-start | bytes 655360 | tf_op jit(solution)/shard_map/all_to_all | solution.py:87
  22.6 0.6 convolution_convert_fusion
  23.2 1.8 collective-permute-start
  25.0 0.8 copy.100
  25.9 0.3 copy.102
  26.3 2.2 collective-permute-done
  28.7 0.3 copy.104
  29.0 741.8 %all-reduce.4.cloned.1.call-done = bf16[1,128,2,8,40]{1,4,3,2,0:T(8,128)(2,1)} async-done(((bf16[1,128,2,8,40]{1,4,3,2,0:T(8,128)(2,1)}), bf16[1,128,2,8,40]{1,4,3,2,0:T(8,128)(2,1)}) %all-reduce.4.cloned.1.call-update) | async-done | bytes 163856 | tf_op jit(solution)/shard_map/psum | solution.py:13
  770.9 1.2 copy.103
  772.0 1.1 pad_maximum_fusion
  773.1 1.0 copy.105
  774.1 27.1 %all-to-all-start = ((bf16[5,128,2,8,40]{1,4,2,0,3:T(8,128)(2,1)}), bf16[5,128,2,8,40]{1,4,2,0,3:T(8,128)(2,1)S(1)}, u32[]{:S(2)}, u32[]{:S(2)}) async-start(bf16[5,128,2,8,40]{1,4,2,0,3:T(8,128)(2,1)} %copy.105), calls=%async_computation | async-start | bytes 1638400 | tf_op jit(solution)/shard_map/all_to_all | solution.py:88
  801.5 20.5 %all-to-all-done = bf16[5,128,2,8,40]{1,4,2,0,3:T(8,128)(2,1)S(1)} async-done(((bf16[5,128,2,8,40]{1,4,2,0,3:T(8,128)(2,1)}), bf16[5,128,2,8,40]{1,4,2,0,3:T(8,128)(2,1)S(1)}, u32[]{:S(2)}, u32[]{:S(2)}) %all-to-all-start) | async-done | bytes 819232 | tf_op jit(solution)/shard_map/all_to_all | solution.py:88
  822.2 19.6 %while.10 = (s32[]{:T(128)}, bf16[4,1024,1,40]{1,3,2,0:T(8,128)(2,1)S(1)}, bf16[4,1024,1,40]{1,3,2,0:T(8,128)(2,1)S(1)}, bf16[1024,1,40]{0,2,1:T(8,128)(2,1)S(1)...) while((s32[]{:T(128)}, ...), condition=%wide.region_6.7_spmd, body=%wide.region_3.6_spmd.sunk | while | flops 353056768 | bytes 26005600 | solution.py:65
  822.3 1.4 multiply_reduce_fusion.4
  823.6 1.9 fusion.91
  825.6 1.5 fusion.92
  827.2 1.4 multiply_reduce_fusion.4
  828.5 1.9 fusion.91
  830.5 1.5 fusion.92
  832.1 1.4 multiply_reduce_fusion.4
  833.4 1.9 fusion.91
  835.4 1.5 fusion.92
  837.0 1.4 multiply_reduce_fusion.4
  838.3 1.9 fusion.91
  840.3 1.5 fusion.92
  841.8 0.7 copy.110
  842.6 2.3 reshape.146
  844.9 4.2 all-to-all-start.2
  849.3 9.8 %all-to-all-done.2 = bf16[8,2,10240]{2,1,0:T(2,128)(2,1)S(1)} async-done(((bf16[8,2,10240]{2,1,0:T(2,128)(2,1)}), bf16[8,2,10240]{2,1,0:T(2,128)(2,1)S(1)}, u32[]{:S(2)}, u32[]{:S(2)}) %all-to-all-start.2) | async-done | bytes 327712 | tf_op jit(solution)/shard_map/all_to_all | solution.py:93
  859.1 1.6 reshape.147
  860.7 0.6 copy.120
  861.3 0.3 copy.112
  861.6 0.4 fusion.36
  862.3 0.3 copy.114
  862.5 0.3 fusion.71
  863.0 14.1 %all-reduce.1 = (f32[4,32]{1,0:T(4,128)S(1)}, f32[4,32]{1,0:T(4,128)S(1)}) all-reduce(f32[4,32]{1,0:T(4,128)S(1)} %copy.116, f32[4,32]{1,0:T(4,128)S(1)} %copy.115), channel_id=1, replica_groups=mesh['frame'=64,'row'=8] {'row'}, use_global_device_ids=true, to_apply=%region_10.11 | all-reduce | flops 256 | bytes 2048 | tf_op jit(solution)/shard_map/psum | solution.py:101
  877.4 0.2 multiply_convert_fusion
  877.7 0.7 fusion.73
  878.4 1.9 collective-permute-start.1
  880.3 2.8 collective-permute-start.2
  883.2 0.2 copy.117
  883.5 0.2 copy.118
  883.8 2.7 collective-permute-done.2
  886.6 1.2 fusion.41
  887.8 0.4 fusion.72
  888.2 1.2 copy-done.2
  889.4 0.4 fusion.58
  889.8 0.4 fusion.49
  890.2 1.0 pad_maximum_fusion.1
  891.2 0.4 convolution_add_fusion.6
  891.6 0.4 convolution_add_fusion.5
  891.9 0.4 convolution_add_fusion.4
  892.3 0.5 convolution_add_fusion.3
  892.9 0.4 convolution_add_fusion.2
  893.3 0.4 convolution_add_fusion.1
  893.7 0.4 fusion.35
  894.1 0.9 copy.119
  (52 shorter events, 2.3 us)
Async XLA Ops:
  6.5 4.6 copy-start
  6.5 16.1 %copy-start.7 = (bf16[320,320]{1,0:T(8,128)(2,1)S(1)}, bf16[320,320]{1,0:T(8,128)(2,1)}, u32[]{:S(2)}) copy-start(bf16[320,320]{1,0:T(8,128)(2,1)} %param.14) | copy-start | bytes 614404
  6.5 16.1 %copy-start.6 = (bf16[320,320]{1,0:T(8,128)(2,1)S(1)}, bf16[320,320]{1,0:T(8,128)(2,1)}, u32[]{:S(2)}) copy-start(bf16[320,320]{1,0:T(8,128)(2,1)} %param.15) | copy-start | bytes 614404
  12.4 761.8 %all-to-all-start.1 = ((bf16[4,128,1,8,40]{1,4,0,2,3:T(8,128)(2,1)}), bf16[4,128,1,8,40]{1,4,0,2,3:T(8,128)(2,1)S(1)}, u32[]{:S(2)}, u32[]{:S(2)}) async-start(bf16[4,128,1,8,40]{1,4,0,2,3:T(8,128)(2,1)} %copy.107), calls=%async_computation.1 | async-start | bytes 655360 | tf_op jit(solution)/shard_map/all_to_all | solution.py:87
  22.6 748.3 %all-reduce.4.cloned.1.call-start = ((), (), s32[]{:S(2)}) async-start(), calls=%async_computation.3 | async-start | bytes 327680 | tf_op jit(solution)/shard_map/psum | solution.py:13
  23.2 5.3 collective-permute-start
  774.1 47.9 %all-to-all-start = ((bf16[5,128,2,8,40]{1,4,2,0,3:T(8,128)(2,1)}), bf16[5,128,2,8,40]{1,4,2,0,3:T(8,128)(2,1)S(1)}, u32[]{:S(2)}, u32[]{:S(2)}) async-start(bf16[5,128,2,8,40]{1,4,2,0,3:T(8,128)(2,1)} %copy.105), calls=%async_computation | async-start | bytes 1638400 | tf_op jit(solution)/shard_map/all_to_all | solution.py:88
  841.8 7.2 copy-start.1
  841.8 7.4 copy-start.4
  844.9 14.2 %all-to-all-start.2 = ((bf16[8,2,10240]{2,1,0:T(2,128)(2,1)}), bf16[8,2,10240]{2,1,0:T(2,128)(2,1)S(1)}, u32[]{:S(2)}, u32[]{:S(2)}) async-start(bf16[8,2,10240]{2,1,0:T(2,128)(2,1)} %reshape.146), calls=%async_computation.2 | async-start | bytes 655360 | tf_op jit(solution)/shard_map/all_to_all | solution.py:93
  849.1 12.6 %copy-start.3 = (bf16[320,320]{1,0:T(8,128)(2,1)S(1)}, bf16[320,320]{1,0:T(8,128)(2,1)}, u32[]{:S(2)}) copy-start(bf16[320,320]{1,0:T(8,128)(2,1)} %param.16) | copy-start | bytes 614404
  862.2 20.9 %copy-start.5 = (bf16[320]{0:T(512)(128)(2,1)S(1)}, bf16[320]{0:T(512)(128)(2,1)}, u32[]{:S(2)}) copy-start(bf16[320]{0:T(512)(128)(2,1)} %param.19) | copy-start | bytes 1924
  878.4 5.4 collective-permute-start.1
  880.3 6.3 collective-permute-start.2
  887.8 1.6 copy-start.2
Sparse Core Ops, SparseCore 0:
  26.3 744.4 all-reduce.3
where the time goes:
time: 902 us
  waiting for transfers between devices  777 us (86%)
  starting transfers between devices  48 us (5%)
  matrix products  16.6 us (2%)
  other arithmetic  16.1 us (2%)
  local copies, waits for them, and re-layouts  15.9 us (2%)
  blocking collectives  14.1 us (2%)
  between operations  13.9 us (2%)
    psum x1, waiting for transfers between devices, spread_2(): return lax.psum(kept, axis)  742 us
    all_to_all x1, starting transfers between devices, body(): lax.all_to_all(sent_pairs, 'row', split_axis=3, concat_axis=1, tiled=True)  27.1 us
    all_to_all x1, waiting for transfers between devices, body(): lax.all_to_all(sent_pairs, 'row', split_axis=3, concat_axis=1, tiled=True)  20.5 us
  transfers between devices with their start and end apart: 7, of which 5 were waited for; matrix products, arithmetic and copies ran while one was open for 1% of the time, Pallas kernels for 0%

commit v1 on v0

--- a/solution.py
+++ b/solution.py
@@ -10,7 +10,7 @@
 
 def spread_2(value, axis, source):
     kept = jnp.where(lax.axis_index(axis) == source, value, 0).astype(value.dtype)
-    return lax.psum(kept, axis)
+    return jnp.sum(lax.all_gather(kept, axis), axis=0)
 
 
 def shifted(block, axis, distance):

time: 902 us -> 359 us (0.40)
  waiting for transfers between devices: 777 us -> 250 us
  starting transfers between devices: 48 us -> 25.7 us
    psum x1 -> x0, waiting for transfers between devices: 742 us -> none  [spread_2(): return lax.psum(kept, axis)]
    all_gather x0 -> x1, waiting for transfers between devices: none -> 214 us  [spread_2(): return jnp.sum(lax.all_gather(kept, axis), axis=0)]
    all_to_all x1, starting transfers between devices: 27.1 us -> 4.6 us  [body(): lax.all_to_all(sent_pairs, 'row', split_axis=3, concat_axis=1, tiled=True)]
  transfers between devices with their start and end apart: 7 -> 7, of which waited for: 5 -> 5; matrix products, arithmetic and copies ran while one was open for 1% -> 3% of each run, Pallas kernels for 0% -> 0%
where the time goes in v1:
time: 359 us; the launch traced here: 358 us
  waiting for transfers between devices  250 us (70%)
  starting transfers between devices  25.7 us (7%)
  other arithmetic  22.5 us (6%)
  matrix products  17.6 us (5%)
  local copies, waits for them, and re-layouts  14.4 us (4%)
  blocking collectives  14.1 us (4%)
  between operations  13.8 us (4%)
    all_gather x1, waiting for transfers between devices, spread_2(): return jnp.sum(lax.all_gather(kept, axis), axis=0)  214 us
    all_to_all x1, waiting for transfers between devices, body(): lax.all_to_all(sent_pairs, 'row', split_axis=3, concat_axis=1, tiled=True)  20.6 us
    psum x1, blocking collectives, body(): group_sum, group_square = lax.psum((sum_parts, square_parts), 'row')  14.1 us
    all_to_all x1, starting transfers between devices, body(): lax.all_to_all(sent_queries, 'row', split_axis=3, concat_axis=1, tiled=True)  10.2 us
    all_to_all x1, waiting for transfers between devices, body(): lax.all_to_all(head_results, 'row', split_axis=1, concat_axis=2, tiled=True)  9.84 us
    reduce_sum x4, other arithmetic, single(): totals = jnp.sum(raised, axis=-1)  7.73 us
  transfers between devices with their start and end apart: 7, of which 5 were waited for; matrix products, arithmetic and copies ran while one was open for 3% of the time, Pallas kernels for 0%

profile of v1, /device:TPU:1, one launch (start us, length us, event | category | flops | bytes accessed | tf_op | source)
XLA Modules:
  0.0 358.4 jit_solution(12490510962905152881)
XLA Ops:
  6.5 1.2 convert_reduce_fusion
  7.7 1.3 multiply_reduce_fusion.1
  9.2 0.7 convert_element_type.65
  9.9 1.2 multiply_convert_fusion.1
  11.1 1.6 convolution_convert_fusion
  12.8 0.7 broadcast_select_fusion.1
  13.5 0.4 convolution_convert_fusion.1
  14.0 0.8 copy.105
  14.7 10.2 %all-to-all-start.1 = ((bf16[4,128,1,8,40]{1,4,0,2,3:T(8,128)(2,1)}), bf16[4,128,1,8,40]{1,4,0,2,3:T(8,128)(2,1)S(1)}, u32[]{:S(2)}, u32[]{:S(2)}) async-start(bf16[4,128,1,8,40]{1,4,0,2,3:T(8,128)(2,1)} %copy.105), calls=%async_computation.1 | async-start | bytes 655360 | tf_op jit(solution)/shard_map/all_to_all | solution.py:87
  24.9 1.7 collective-permute-start
  26.8 0.3 copy.100
  27.2 3.1 collective-permute-done
  30.5 0.3 copy.102
  30.8 214.0 %all-gather.3.cloned.1.call-done = bf16[8192,640]{1,0:T(8,128)(2,1)} async-done(((bf16[128,640]{1,0:T(8,128)(2,1)}), bf16[8192,640]{1,0:T(8,128)(2,1)}) %all-gather.3.cloned.1.call-update) | async-done | bytes 10485776 | tf_op jit(solution)/shard_map/all_gather | solution.py:13
  244.8 5.8 %reduce_sum.59 = bf16[128,640]{1,0:T(8,128)(2,1)S(1)} reduce(bf16[64,128,640]{2,1,0:T(8,128)(2,1)} %bitcast.143, bf16[]{:T(256)} %constant.37.clone.1), dimensions={0}, to_apply=%region_2.3 | reduce | flops 5160960 | bytes 10649602 | tf_op jit(solution)/shard_map/reduce_sum | solution.py:13
  250.7 0.3 copy.101
  251.0 1.1 pad_maximum_fusion
  252.1 1.0 copy.103
  253.1 4.6 %all-to-all-start = ((bf16[5,128,2,8,40]{1,4,2,0,3:T(8,128)(2,1)}), bf16[5,128,2,8,40]{1,4,2,0,3:T(8,128)(2,1)S(1)}, u32[]{:S(2)}, u32[]{:S(2)}) async-start(bf16[5,128,2,8,40]{1,4,2,0,3:T(8,128)(2,1)} %copy.103), calls=%async_computation | async-start | bytes 1638400 | tf_op jit(solution)/shard_map/all_to_all | solution.py:88
  258.0 20.6 %all-to-all-done = bf16[5,128,2,8,40]{1,4,2,0,3:T(8,128)(2,1)S(1)} async-done(((bf16[5,128,2,8,40]{1,4,2,0,3:T(8,128)(2,1)}), bf16[5,128,2,8,40]{1,4,2,0,3:T(8,128)(2,1)S(1)}, u32[]{:S(2)}, u32[]{:S(2)}) %all-to-all-start) | async-done | bytes 819232 | tf_op jit(solution)/shard_map/all_to_all | solution.py:88
  278.7 19.6 %while.10 = (s32[]{:T(128)}, bf16[4,1024,1,40]{1,3,2,0:T(8,128)(2,1)S(1)}, bf16[4,1024,1,40]{1,3,2,0:T(8,128)(2,1)S(1)}, bf16[1024,1,40]{0,2,1:T(8,128)(2,1)S(1)...) while((s32[]{:T(128)}, ...), condition=%wide.region_6.7_spmd, body=%wide.region_3.6_spmd.sunk | while | flops 353056768 | bytes 26005600 | solution.py:65
  278.8 1.4 multiply_reduce_fusion.4
  280.1 1.9 fusion.91
  282.1 1.5 fusion.92
  283.7 1.4 multiply_reduce_fusion.4
  285.0 1.9 fusion.91
  287.0 1.5 fusion.92
  288.5 1.4 multiply_reduce_fusion.4
  289.9 1.9 fusion.91
  291.9 1.5 fusion.92
  293.4 1.4 multiply_reduce_fusion.4
  294.8 1.9 fusion.91
  296.7 1.5 fusion.92
  298.3 0.7 copy.108
  299.1 2.3 reshape.147
  301.3 4.2 %all-to-all-start.2 = ((bf16[8,2,10240]{2,1,0:T(2,128)(2,1)}), bf16[8,2,10240]{2,1,0:T(2,128)(2,1)S(1)}, u32[]{:S(2)}, u32[]{:S(2)}) async-start(bf16[8,2,10240]{2,1,0:T(2,128)(2,1)} %reshape.147), calls=%async_computation.2 | async-start | bytes 655360 | tf_op jit(solution)/shard_map/all_to_all | solution.py:93
  305.8 9.8 %all-to-all-done.2 = bf16[8,2,10240]{2,1,0:T(2,128)(2,1)S(1)} async-done(((bf16[8,2,10240]{2,1,0:T(2,128)(2,1)}), bf16[8,2,10240]{2,1,0:T(2,128)(2,1)S(1)}, u32[]{:S(2)}, u32[]{:S(2)}) %all-to-all-start.2) | async-done | bytes 327712 | tf_op jit(solution)/shard_map/all_to_all | solution.py:93
  315.6 1.6 reshape.148
  317.2 0.6 copy.118
  317.8 0.3 copy.110
  318.1 0.4 fusion.36
  318.8 0.3 copy.112
  319.0 0.3 fusion.71
  319.5 14.1 %all-reduce.1 = (f32[4,32]{1,0:T(4,128)S(1)}, f32[4,32]{1,0:T(4,128)S(1)}) all-reduce(f32[4,32]{1,0:T(4,128)S(1)} %copy.114, f32[4,32]{1,0:T(4,128)S(1)} %copy.113), channel_id=1, replica_groups=mesh['frame'=64,'row'=8] {'row'}, use_global_device_ids=true, to_apply=%region_10.11 | all-reduce | flops 256 | bytes 2048 | tf_op jit(solution)/shard_map/psum | solution.py:101
  334.0 0.2 multiply_convert_fusion
  334.2 0.7 fusion.73
  334.9 1.9 collective-permute-start.1
  336.8 3.1 collective-permute-start.2
  340.0 0.2 copy.115
  340.5 2.5 collective-permute-done.2
  343.1 1.2 fusion.41
  344.3 0.4 fusion.72
  344.7 1.2 copy-done.2
  345.9 0.4 fusion.58
  346.3 0.4 fusion.49
  346.7 1.0 pad_maximum_fusion.1
  347.7 0.4 convolution_add_fusion.6
  348.1 0.4 convolution_add_fusion.5
  348.5 0.4 convolution_add_fusion.4
  348.9 0.5 convolution_add_fusion.3
  349.4 0.4 convolution_add_fusion.2
  349.8 0.4 convolution_add_fusion.1
  350.2 0.4 fusion.35
  350.6 0.9 copy.117
  (49 shorter events, 2.7 us)
Async XLA Ops:
  6.5 6.9 %copy-start = (bf16[320,320]{1,0:T(8,128)(2,1)S(1)}, bf16[320,320]{1,0:T(8,128)(2,1)}, u32[]{:S(2)}) copy-start(bf16[320,320]{1,0:T(8,128)(2,1)} %param.13) | copy-start | bytes 614404
  6.5 238.2 %all-gather.3.cloned.1.call-start = ((), (), s32[]{:S(2)}) async-start(), calls=%async_computation.3 | async-start | bytes 10649600 | tf_op jit(solution)/shard_map/all_gather | solution.py:13
  14.7 238.4 %all-to-all-start.1 = ((bf16[4,128,1,8,40]{1,4,0,2,3:T(8,128)(2,1)}), bf16[4,128,1,8,40]{1,4,0,2,3:T(8,128)(2,1)S(1)}, u32[]{:S(2)}, u32[]{:S(2)}) async-start(bf16[4,128,1,8,40]{1,4,0,2,3:T(8,128)(2,1)} %copy.105), calls=%async_computation.1 | async-start | bytes 655360 | tf_op jit(solution)/shard_map/all_to_all | solution.py:87
  24.9 5.4 %collective-permute-start = (bf16[128,640]{1,0:T(8,128)(2,1)S(1)}, bf16[128,640]{1,0:T(8,128)(2,1)S(1)}, u32[]{:S(2)}, u32[]{:S(2)}) collective-permute-start(bf16[128,640]{1,0:T(8,128)(2,1)S(1)} %get-tuple-element.118), channel_id=1, source_target_pairs={{0,8},{8,16},{16,24},{24,32},{32,40},{40,48},{48,56},{56,64},{64,7... | collective-permute-start | bytes 491528 | tf_op jit(solution)/shard_map/ppermute | solution.py:19
  253.1 25.4 %all-to-all-start = ((bf16[5,128,2,8,40]{1,4,2,0,3:T(8,128)(2,1)}), bf16[5,128,2,8,40]{1,4,2,0,3:T(8,128)(2,1)S(1)}, u32[]{:S(2)}, u32[]{:S(2)}) async-start(bf16[5,128,2,8,40]{1,4,2,0,3:T(8,128)(2,1)} %copy.103), calls=%async_computation | async-start | bytes 1638400 | tf_op jit(solution)/shard_map/all_to_all | solution.py:88
  298.3 7.3 %copy-start.1 = (bf16[4,4,32,320]{3,2,1,0:T(8,128)(2,1)S(1)}, bf16[4,4,32,320]{3,2,1,0:T(8,128)(2,1)}, u32[]{:S(2)}) copy-start(bf16[4,4,32,320]{3,2,1,0:T(8,128)(2,1)} %param.11) | copy-start | bytes 983044
  298.3 7.4 %copy-start.4 = (bf16[320]{0:T(512)(128)(2,1)S(1)}, bf16[320]{0:T(512)(128)(2,1)}, u32[]{:S(2)}) copy-start(bf16[320]{0:T(512)(128)(2,1)} %param.17) | copy-start | bytes 1924
  301.3 14.3 %all-to-all-start.2 = ((bf16[8,2,10240]{2,1,0:T(2,128)(2,1)}), bf16[8,2,10240]{2,1,0:T(2,128)(2,1)S(1)}, u32[]{:S(2)}, u32[]{:S(2)}) async-start(bf16[8,2,10240]{2,1,0:T(2,128)(2,1)} %reshape.147), calls=%async_computation.2 | async-start | bytes 655360 | tf_op jit(solution)/shard_map/all_to_all | solution.py:93
  305.6 12.6 %copy-start.3 = (bf16[320,320]{1,0:T(8,128)(2,1)S(1)}, bf16[320,320]{1,0:T(8,128)(2,1)}, u32[]{:S(2)}) copy-start(bf16[320,320]{1,0:T(8,128)(2,1)} %param.16) | copy-start | bytes 614404
  318.7 21.1 %copy-start.5 = (bf16[320]{0:T(512)(128)(2,1)S(1)}, bf16[320]{0:T(512)(128)(2,1)}, u32[]{:S(2)}) copy-start(bf16[320]{0:T(512)(128)(2,1)} %param.19) | copy-start | bytes 1924
  334.9 5.6 %collective-permute-start.1 = (bf16[4,1,32,320]{3,2,1,0:T(8,128)(2,1)}, bf16[4,1,32,320]{3,2,1,0:T(8,128)(2,1)S(1)}, u32[]{:S(2)}, u32[]{:S(2)}) collective-permute-start(bf16[4,1,32,320]{3,2,1,0:T(8,128)(2,1)} %get-tuple-element.121), channel_id=1, source_target_pairs={{0,1},{1,2},{2,3},{3,4},{4,5},{5,6},{6,7},{8,9},{9,10},{10,11},{11... | collective-permute-start | bytes 245768 | tf_op jit(solution)/shard_map/ppermute | solution.py:29
  336.8 6.3 %collective-permute-start.2 = (bf16[4,1,32,320]{3,2,1,0:T(8,128)(2,1)}, bf16[4,1,32,320]{3,2,1,0:T(8,128)(2,1)}, u32[]{:S(2)}, u32[]{:S(2)}) collective-permute-start(bf16[4,1,32,320]{3,2,1,0:T(8,128)(2,1)} %get-tuple-element.122), channel_id=1, source_target_pairs={{1,0},{2,1},{3,2},{4,3},{5,4},{6,5},{7,6},{9,8},{10,9},{11,10},{12... | collective-permute-start | bytes 245768 | tf_op jit(solution)/shard_map/ppermute | solution.py:30
  344.3 1.6 copy-start.2
Sparse Core Ops, SparseCore 0:
  13.6 231.1 all-gather.2
